TPU v7x, 128 devices: a whole 4x4x4 slice. The times are simulated.
128 devices in a mesh: field: 2 (over x_lo), row: 8 (over z, core), col: 8 (over x_hi, y).
Axes of the slice: x: 4 (x_hi: 2, x_lo: 2; x = x_hi * 2 + x_lo), y: 4, z: 4, core: 2. Of those that a mesh axis runs over, the one named last changes fastest.
Arguments:
- init_state: float32 [2, 4, 2048, 4096], P('field', None, 'row', 'col'), may hold values from 0 to 2
- cond_x: float32 [2, 4, 2048, 4096], P('field', None, 'row', 'col'), may hold values from 0.2 to 2
- cond_y: float32 [2, 4, 2048, 4096], P('field', None, 'row', 'col'), may hold values from 0.2 to 2
- activity: float32 [2, 2048, 4096], P('field', 'row', 'col'), may hold values from 0.5 to 1.5
- power_class: int32 [2, 2048, 4096], P('field', 'row', 'col'), may hold values from 0 to 7
- class_table: float32 [2, 8], P('field'), may hold values from 0.25 to 2
- via_mask: int32 [2, 3, 2048, 4096], P('field', None, 'row', 'col'), may hold values 0 or 1
Outputs:
- final_state: float32 [2, 4, 2048, 4096], P('field', None, 'row', 'col')
All inputs are finite; a program needn't handle non-finite values. No bound on the sum of `via_mask` on one device may be relied on, other than what follows from the above.
Results may differ from a plain program's by a relative error of at most 0.00002.
Values sent between devices are 32-bit elements; how exact they have to be, the bound alone decides.
A program may use at most 128 MiB of HBM per device.

v0:
```python
import jax
import jax.numpy as jnp
from jax import lax
from jax.sharding import PartitionSpec as P

SWEEPS = 4
STEPS = 2


LEAK = 0.05
VIA_G = 1.0
TEMP_COEF = 0.5
HEAT_SCALE = 1.0


def with_halo(block, sides, width):
    for axis, dim in sides:
        count = lax.axis_size(axis)
        forward = [(i, i + 1) for i in range(count - 1)]
        backward = [(target, source) for source, target in forward]
        low = lax.ppermute(
            lax.slice_in_dim(block, block.shape[dim] - width, None, axis=dim), axis, forward
        )
        high = lax.ppermute(lax.slice_in_dim(block, 0, width, axis=dim), axis, backward)
        block = jnp.concatenate([low, block, high], axis=dim)
    return block


def from_partner(shard, axis, distance):
    return lax.ppermute(shard, axis, [(i, i ^ 1 << distance) for i in range(lax.axis_size(axis))])


def trim_rim(array_in, amount):
    return array_in[:, amount : array_in.shape[1] - amount, amount : array_in.shape[2] - amount]


def face_average(kappa, valid, axis_index):
    if axis_index == 2:
        following = jnp.concatenate([kappa[:, :, 1:], jnp.zeros_like(kappa[:, :, :1])], 2)
        return 0.5 * (kappa + following) * valid[None, None, :]
    following = jnp.concatenate([kappa[:, 1:, :], jnp.zeros_like(kappa[:, :1, :])], 1)
    return 0.5 * (kappa + following) * valid[None, :, None]


def sweep_once(padded, cond_e, cond_s, source, vertical):
    center = padded[:, 1:-1, 1:-1]
    east_value = padded[:, 1:-1, 2:]
    west_value = padded[:, 1:-1, :-2]
    south_value = padded[:, 2:, 1:-1]
    north_value = padded[:, :-2, 1:-1]
    cond_east = cond_e[:, 1:-1, 1:-1]
    cond_west = cond_e[:, 1:-1, :-2]
    cond_south = cond_s[:, 1:-1, 1:-1]
    cond_north = cond_s[:, :-2, 1:-1]
    source_in = source[:, 1:-1, 1:-1]
    vert_in = vertical[:, 1:-1, 1:-1]
    zero_plane = jnp.zeros_like(center[:1])
    link_up = jnp.concatenate([zero_plane, vert_in], 0)
    link_down = jnp.concatenate([vert_in, zero_plane], 0)
    above = jnp.concatenate([zero_plane, center[:-1]], 0)
    below = jnp.concatenate([center[1:], zero_plane], 0)
    total = (
        source_in
        + cond_east * east_value
        + cond_west * west_value
        + cond_south * south_value
        + cond_north * north_value
        + link_up * above
        + link_down * below
    )
    weight = cond_east + cond_west + cond_south + cond_north + link_up + link_down + LEAK
    return total / weight


def relax(padded, coefficients, inside_mask):
    current = padded
    trimmed = [trim_rim(member, 0) for member in coefficients]
    current = sweep_once(current, trimmed[0], trimmed[1], trimmed[2], trimmed[3])
    current = current * trim_rim(inside_mask, 1)
    return current


def shards(init_state, cond_x, cond_y, activity, power_class, class_table, via_mask):
    halo_depth = 1
    is_elec = lax.axis_index("field") == 0
    state = init_state[0]
    rows_here = state.shape[1]
    cols_here = state.shape[2]
    class_ids = jnp.arange(class_table.shape[1], dtype=jnp.int32)
    density = jnp.sum(
        jnp.where(
            power_class[0][None] == class_ids[:, None, None], class_table[0][:, None, None], 0.0
        ),
        axis=0,
    )
    load = density * activity[0]
    plane_select = jnp.where(
        is_elec,
        jnp.array([0.0, 1.0, 1.0, 0.0], jnp.float32),
        jnp.array([0.0, 1.0, 0.0, 0.0], jnp.float32),
    )
    face_select = jnp.where(
        is_elec, jnp.array([1.0, 0.0, 1.0], jnp.float32), jnp.array([1.0, 1.0, 1.0], jnp.float32)
    )
    base = plane_select[:, None, None] * load[None]
    vertical = via_mask[0].astype(jnp.float32) * VIA_G * face_select[:, None, None]
    statics = jnp.concatenate([cond_x[0], cond_y[0], base, vertical], 0)
    widened = with_halo(statics, (("row", 1), ("col", 2)), halo_depth)
    cond_e_wide = widened[0:4]
    cond_s_wide = widened[4:8]
    base_wide = widened[8:12]
    vert_wide = widened[12:15]
    total_rows = rows_here * lax.axis_size("row")
    total_cols = cols_here * lax.axis_size("col")
    row_ids = (
        lax.axis_index("row") * rows_here
        - halo_depth
        + jnp.arange(rows_here + 2 * halo_depth, dtype=jnp.int32)
    )
    col_ids = (
        lax.axis_index("col") * cols_here
        - halo_depth
        + jnp.arange(cols_here + 2 * halo_depth, dtype=jnp.int32)
    )
    inside_rows = (row_ids >= 0) & (row_ids < total_rows)
    inside_cols = (col_ids >= 0) & (col_ids < total_cols)
    inside_mask = (inside_rows[:, None] & inside_cols[None, :]).astype(jnp.float32)[None]
    south_valid = ((row_ids >= 0) & (row_ids + 1 < total_rows)).astype(jnp.float32)
    east_valid = ((col_ids >= 0) & (col_ids + 1 < total_cols)).astype(jnp.float32)
    plane_map = jnp.array([0, 1, 1, 0], jnp.int32)
    near_e = trim_rim(cond_e_wide, halo_depth - 1)
    near_s = trim_rim(cond_s_wide, halo_depth - 1)
    for step_index in range(STEPS):
        coefficients = None
        for group_index in range(SWEEPS // halo_depth):
            extra_rim = 0
            deeper = with_halo(state, (("row", 1), ("col", 2)), halo_depth + extra_rim)
            padded = trim_rim(deeper, extra_rim)
            if group_index == 0:
                near = trim_rim(padded, halo_depth - 1)
                middle = near[:, 1:-1, 1:-1]
                heat = (
                    near_e[:, 1:-1, 1:-1] * (middle - near[:, 1:-1, 2:]) ** 2
                    + near_s[:, 1:-1, 1:-1] * (middle - near[:, 2:, 1:-1]) ** 2
                )
                outgoing = jnp.where(
                    is_elec, jnp.stack([heat[0] + heat[3], heat[1] + heat[2]]), middle[0:2]
                )
                incoming = from_partner(outgoing, "field", 0)
                incoming_wide = with_halo(incoming, (("row", 1), ("col", 2)), halo_depth)
                factor = jnp.where(is_elec, 1.0 / (1.0 + TEMP_COEF * incoming_wide[plane_map]), 1.0)
                heat_planes = jnp.concatenate([incoming_wide, jnp.zeros_like(incoming_wide)], 0)
                source_now = base_wide + jnp.where(is_elec, 0.0, HEAT_SCALE * heat_planes)
                link_east = face_average(cond_e_wide * factor, east_valid, 2)
                link_south = face_average(cond_s_wide * factor, south_valid, 1)
                coefficients = (link_east, link_south, source_now, vert_wide)
            state = relax(padded, coefficients, inside_mask)
    return state[None]


def solution(mesh):
    return jax.shard_map(
        shards,
        mesh=mesh,
        in_specs=(
            P("field", None, "row", "col"),
            P("field", None, "row", "col"),
            P("field", None, "row", "col"),
            P("field", "row", "col"),
            P("field", "row", "col"),
            P("field", None),
            P("field", None, "row", "col"),
        ),
        out_specs=P("field", None, "row", "col"),
        check_vma=False,
    )
```

profile of v0, /device:TPU:25, one launch (start us, length us, event | category | flops | bytes accessed | tf_op | source)
XLA Modules:
  0.0 450.9 jit_solution(16469260032062597412)
XLA Ops:
  23.9 5.4 %collective-permute-done.6 = f32[4,258,1]{1,0,2:T(4,128)S(1)} collective-permute-done((f32[4,258,1]{1,0,2:T(4,128)S(1)}, f32[4,258,1]{1,0,2:T(4,128)S(1)}, u32[]{:S(2)}, u32[]{:S(2)}) %collective-permute-start.6) | collective-permute-done | bytes 4160 | tf_op jit(solution)/shard_map/ppermute | solution.py:24
  29.6 5.6 %fusion.104 = f32[4,256,512]{2,1,0:T(8,128)S(1)} fusion(f32[4,256,512]{2,1,0:T(8,128)} %bitcast.29, f32[4,1,512]{2,1,0:T(1,128)S(1)} %copy.145, f32[4,258,1]{2,1,0:T(8,128)S(1)} %copy.147, f32[4,1,512]{2,1,0:T(1,128)S(1)} %copy.144, f32[1,4,256,512]{3,2,1,0:T(8,128)} %param.14, f32[1,4,256,512]{3,2,1,0:T(8,128)} %param.13), kind=kLoop, calls=%fused_computation.202 | loop fusion | flops 5767168 | bytes 8409120 | tf_op jit(solution)/shard_map/add | solution.py:143
  44.4 4.5 pad_maximum_fusion.70
  59.0 4.4 collective-permute-done.7
  63.4 4.1 collective-permute-start.8
  80.4 14.9 %pad_maximum_fusion = f32[15,258,514]{2,1,0:T(8,128)} fusion(f32[15,258,1]{2,1,0:T(8,128)} %copy.141, f32[15,1,512]{2,1,0:T(1,128)S(1)} %collective-permute-done.1, f32[3,256,512]{2,1,0:T(8,128)S(1)} %bitcast_multiply_fusion, f32[4,256,512]{2,1,0:T(8,128)} %copy-done.19, f32[4,256,512]{2,1,0:T(8,128)} %bitcast.32, f32[4,256,512]{2,1,0:T(8,128)} %bitcast.35, ...), kind=kLoop, calls=%fused_computation.2 | loop fusion | flops 13924260 | bytes 15913440 | tf_op jit(solution)/shard_map/concatenate | solution.py:25
  98.2 4.8 %slice_multiply_fusion.3 = (f32[4,258,514]{2,1,0:T(8,128)S(1)}, f32[4,258,514]{2,1,0:T(8,128)S(1)}, f32[4,258,514]{2,1,0:T(8,128)S(1)}) fusion(f32[15,258,514]{2,1,0:T(8,128)} %pad_maximum_fusion, f32[4,258,514]{2,1,0:T(8,128)} %gather_fusion, pred[]{:T(512)S(6)} %eq.18), kind=kLoop, calls=%fused_computation.34 | loop fusion | flops 3182688 | bytes 14852545 | tf_op jit(solution)/shard_map/mul | solution.py:154
  108.3 9.0 %fusion.3 = f32[4,256,512]{2,1,0:T(8,128)S(1)} fusion(f32[3,256,512]{2,1,0:T(8,128)S(1)} %bitcast_multiply_fusion, f32[4,256,512]{2,1,0:T(8,128)S(1)} %bitcast.30, f32[4,1,512]{2,1,0:T(1,128)S(1)} %copy.144, f32[4,258,1]{2,1,0:T(8,128)} %copy.150, f32[4,1,512]{2,1,0:T(1,128)S(1)} %copy.145, f32[3,256,512]{2,1,0:T(8,128)} %get-tuple-element.63, ...), kind=kLoop, calls=%fused_computation.38 | loop fusion | flops 15728640 | bytes 21008480 | tf_op jit(solution)/shard_map/mul | solution.py:79
  117.3 4.2 collective-permute-start.13
  132.3 7.2 %collective-permute-start.16 = (f32[4,258,1]{1,0,2:T(4,128)S(1)}, f32[4,258,1]{1,0,2:T(4,128)S(1)}, u32[]{:S(2)}, u32[]{:S(2)}) collective-permute-start(f32[4,258,1]{1,0,2:T(4,128)S(1)} %copy.158), channel_id=1, source_target_pairs={{0,1},{1,2},{2,3},{3,4},{4,5},{5,6},{6,7},{8,9},{9,10},{10,11},{11... | collective-permute-start | bytes 12392 | tf_op jit(solution)/shard_map/ppermute | solution.py:21
  139.5 4.1 fusion.128
  145.7 12.1 %fusion.7 = f32[4,256,512]{2,1,0:T(8,128)S(1)} fusion(f32[3,256,512]{2,1,0:T(8,128)S(1)} %bitcast_multiply_fusion, f32[4,256,512]{2,1,0:T(8,128)} %copy-done.18, f32[4,1,512]{2,1,0:T(1,128)S(1)} %copy.154, f32[4,1,512]{2,1,0:T(1,128)S(1)} %copy.155, f32[4,258,1]{2,1,0:T(8,128)} %copy.159, f32[4,258,1]{2,1,0:T(8,128)} %copy.157, ...), kind=kLoop, calls=%fused_computation.42 | loop fusion | flops 15728640 | bytes 21008480 | tf_op jit(solution)/shard_map/mul | solution.py:79
  171.1 7.0 %collective-permute-start.20 = (f32[4,258,1]{1,0,2:T(4,128)S(1)}, f32[4,258,1]{1,0,2:T(4,128)S(1)}, u32[]{:S(2)}, u32[]{:S(2)}) collective-permute-start(f32[4,258,1]{1,0,2:T(4,128)S(1)} %copy.168), channel_id=1, source_target_pairs={{0,1},{1,2},{2,3},{3,4},{4,5},{5,6},{6,7},{8,9},{9,10},{10,11},{11... | collective-permute-start | bytes 12392 | tf_op jit(solution)/shard_map/ppermute | solution.py:21
  178.1 4.1 fusion.126
  184.3 12.1 %fusion.11 = f32[4,256,512]{2,1,0:T(8,128)S(1)} fusion(f32[3,256,512]{2,1,0:T(8,128)S(1)} %bitcast_multiply_fusion, f32[4,256,512]{2,1,0:T(8,128)} %copy-done.15, f32[4,1,512]{2,1,0:T(1,128)S(1)} %copy.164, f32[4,1,512]{2,1,0:T(1,128)S(1)} %copy.165, f32[4,258,1]{2,1,0:T(8,128)} %copy.169, f32[4,258,1]{2,1,0:T(8,128)} %copy.167, ...), kind=kLoop, calls=%fused_computation.46 | loop fusion | flops 15728640 | bytes 21008480 | tf_op jit(solution)/shard_map/mul | solution.py:79
  209.7 7.4 %collective-permute-start.24 = (f32[4,258,1]{1,0,2:T(4,128)S(1)}, f32[4,258,1]{1,0,2:T(4,128)S(1)}, u32[]{:S(2)}, u32[]{:S(2)}) collective-permute-start(f32[4,258,1]{1,0,2:T(4,128)S(1)} %copy.178), channel_id=1, source_target_pairs={{0,1},{1,2},{2,3},{3,4},{4,5},{5,6},{6,7},{8,9},{9,10},{10,11},{11... | collective-permute-start | bytes 12392 | tf_op jit(solution)/shard_map/ppermute | solution.py:21
  217.1 4.1 fusion.124
  223.3 12.1 %fusion.15 = f32[4,256,512]{2,1,0:T(8,128)S(1)} fusion(f32[3,256,512]{2,1,0:T(8,128)S(1)} %bitcast_multiply_fusion, f32[4,256,512]{2,1,0:T(8,128)} %copy-done.14, f32[4,1,512]{2,1,0:T(1,128)S(1)} %copy.174, f32[4,1,512]{2,1,0:T(1,128)S(1)} %copy.175, f32[4,258,1]{2,1,0:T(8,128)} %copy.179, f32[4,258,1]{2,1,0:T(8,128)} %copy.177, ...), kind=kLoop, calls=%fused_computation.50 | loop fusion | flops 15728640 | bytes 21008480 | tf_op jit(solution)/shard_map/mul | solution.py:79
  246.2 6.1 %collective-permute-done.27 = f32[4,258,1]{1,0,2:T(4,128)S(1)} collective-permute-done((f32[4,258,1]{1,0,2:T(4,128)S(1)}, f32[4,258,1]{1,0,2:T(4,128)S(1)}, u32[]{:S(2)}, u32[]{:S(2)}) %collective-permute-start.27) | collective-permute-done | bytes 4160 | tf_op jit(solution)/shard_map/ppermute | solution.py:24
  252.5 5.6 %fusion.69 = f32[4,256,512]{2,1,0:T(8,128)S(1)} fusion(f32[4,256,512]{2,1,0:T(8,128)} %copy-done.6, f32[4,1,512]{2,1,0:T(1,128)S(1)} %copy.185, f32[4,258,1]{2,1,0:T(8,128)S(1)} %copy.187, f32[4,1,512]{2,1,0:T(1,128)S(1)} %copy.184, f32[1,4,256,512]{3,2,1,0:T(8,128)} %param.14, f32[1,4,256,512]{3,2,1,0:T(8,128)} %param.13), kind=kLoop, calls=%fused_computation.134 | loop fusion | flops 5767168 | bytes 8409120 | tf_op jit(solution)/shard_map/add | solution.py:143
  260.6 24.0 %collective-permute-done.28 = f32[2,256,512]{2,1,0:T(8,128)S(1)} collective-permute-done((f32[2,256,512]{2,1,0:T(8,128)S(1)}, f32[2,256,512]{2,1,0:T(8,128)S(1)}, u32[]{:S(2)}, u32[]{:S(2)}) %collective-permute-start.28) | collective-permute-done | bytes 1048608 | tf_op jit(solution)/shard_map/ppermute | solution.py:30
  323.9 7.0 %fusion.19 = f32[4,256,512]{2,1,0:T(8,128)S(1)} fusion(f32[3,256,512]{2,1,0:T(8,128)S(1)} %bitcast_multiply_fusion, f32[4,256,512]{2,1,0:T(8,128)S(1)} %copy-done.8, f32[4,1,512]{2,1,0:T(1,128)S(1)} %copy.184, f32[4,258,1]{2,1,0:T(8,128)S(1)} %copy-done.29, f32[4,1,512]{2,1,0:T(1,128)S(1)} %copy.185, f32[3,256,512]{2,1,0:T(8,128)S(1)} %copy-done.22, ...), kind=kLoop, calls=%fused_computation.54 | loop fusion | flops 15728640 | bytes 21008480 | tf_op jit(solution)/shard_map/mul | solution.py:79
  330.9 4.5 collective-permute-start.34
  346.1 7.0 %collective-permute-start.37 = (f32[4,258,1]{1,0,2:T(4,128)S(1)}, f32[4,258,1]{1,0,2:T(4,128)S(1)}, u32[]{:S(2)}, u32[]{:S(2)}) collective-permute-start(f32[4,258,1]{1,0,2:T(4,128)S(1)} %copy.198), channel_id=1, source_target_pairs={{0,1},{1,2},{2,3},{3,4},{4,5},{5,6},{6,7},{8,9},{9,10},{10,11},{11... | collective-permute-start | bytes 12392 | tf_op jit(solution)/shard_map/ppermute | solution.py:21
  353.1 4.2 fusion.120
  359.4 12.3 %fusion.23 = f32[4,256,512]{2,1,0:T(8,128)S(1)} fusion(f32[3,256,512]{2,1,0:T(8,128)S(1)} %bitcast_multiply_fusion, f32[4,256,512]{2,1,0:T(8,128)} %copy-done.16, f32[4,1,512]{2,1,0:T(1,128)S(1)} %copy.194, f32[4,1,512]{2,1,0:T(1,128)S(1)} %copy.195, f32[4,258,1]{2,1,0:T(8,128)} %copy.199, f32[4,258,1]{2,1,0:T(8,128)} %copy.197, ...), kind=kLoop, calls=%fused_computation.58 | loop fusion | flops 15728640 | bytes 21008480 | tf_op jit(solution)/shard_map/mul | solution.py:79
  385.0 7.2 %collective-permute-start.41 = (f32[4,258,1]{1,0,2:T(4,128)S(1)}, f32[4,258,1]{1,0,2:T(4,128)S(1)}, u32[]{:S(2)}, u32[]{:S(2)}) collective-permute-start(f32[4,258,1]{1,0,2:T(4,128)S(1)} %copy.208), channel_id=1, source_target_pairs={{0,1},{1,2},{2,3},{3,4},{4,5},{5,6},{6,7},{8,9},{9,10},{10,11},{11... | collective-permute-start | bytes 12392 | tf_op jit(solution)/shard_map/ppermute | solution.py:21
  392.2 4.2 fusion.118
  398.6 12.3 %fusion.27 = f32[4,256,512]{2,1,0:T(8,128)S(1)} fusion(f32[3,256,512]{2,1,0:T(8,128)S(1)} %bitcast_multiply_fusion, f32[4,256,512]{2,1,0:T(8,128)} %copy-done.17, f32[4,1,512]{2,1,0:T(1,128)S(1)} %copy.204, f32[4,1,512]{2,1,0:T(1,128)S(1)} %copy.205, f32[4,258,1]{2,1,0:T(8,128)} %copy.209, f32[4,258,1]{2,1,0:T(8,128)} %copy.207, ...), kind=kLoop, calls=%fused_computation.62 | loop fusion | flops 15728640 | bytes 21008480 | tf_op jit(solution)/shard_map/mul | solution.py:79
  424.1 7.0 %collective-permute-start.45 = (f32[4,258,1]{1,0,2:T(4,128)S(1)}, f32[4,258,1]{1,0,2:T(4,128)S(1)}, u32[]{:S(2)}, u32[]{:S(2)}) collective-permute-start(f32[4,258,1]{1,0,2:T(4,128)S(1)} %copy.218), channel_id=1, source_target_pairs={{0,1},{1,2},{2,3},{3,4},{4,5},{5,6},{6,7},{8,9},{9,10},{10,11},{11... | collective-permute-start | bytes 12392 | tf_op jit(solution)/shard_map/ppermute | solution.py:21
  431.1 4.2 fusion.116
  437.5 13.2 %fusion.32 = f32[1,4,256,512]{3,2,1,0:T(8,128)} fusion(f32[3,256,512]{2,1,0:T(8,128)S(1)} %bitcast_multiply_fusion, f32[4,256,512]{2,1,0:T(8,128)} %copy-done.13, f32[4,1,512]{2,1,0:T(1,128)S(1)} %copy.214, f32[4,1,512]{2,1,0:T(1,128)S(1)} %copy.215, f32[4,258,1]{2,1,0:T(8,128)} %copy.219, f32[4,258,1]{2,1,0:T(8,128)} %copy.217, ...), kind=kLoop, calls=%fused_computation.67 | loop fusion | flops 15728640 | bytes 21008480 | tf_op jit(solution)/shard_map/broadcast_in_dim | solution.py:158
  (274 shorter events, 203.4 us)
Async XLA Ops:
  1.0 17.8 %collective-permute-start.4 = (f32[4,1,512]{2,0,1:T(4,128)S(1)}, f32[4,1,512]{2,0,1:T(4,128)S(1)}, u32[]{:S(2)}, u32[]{:S(2)}) collective-permute-start(f32[4,1,512]{2,0,1:T(4,128)S(1)} %copy.142), channel_id=1, source_target_pairs={{0,8},{8,16},{16,24},{24,32},{32,40},{40,48},{48,56},{1,9},{9,17},... | collective-permute-start | bytes 24584 | tf_op jit(solution)/shard_map/ppermute | solution.py:21
  5.1 13.7 %collective-permute-start.5 = (f32[4,1,512]{2,0,1:T(4,128)S(1)}, f32[4,1,512]{2,0,1:T(4,128)S(1)}, u32[]{:S(2)}, u32[]{:S(2)}) collective-permute-start(f32[4,1,512]{2,0,1:T(4,128)S(1)} %copy.143), channel_id=1, source_target_pairs={{8,0},{16,8},{24,16},{32,24},{40,32},{48,40},{56,48},{9,1},{17,9},... | collective-permute-start | bytes 24584 | tf_op jit(solution)/shard_map/ppermute | solution.py:24
  13.2 31.2 %collective-permute-start = (f32[15,1,512]{2,1,0:T(1,128)S(1)}, f32[15,1,512]{2,1,0:T(1,128)S(1)}, u32[]{:S(2)}, u32[]{:S(2)}) collective-permute-start(f32[15,1,512]{2,1,0:T(1,128)S(1)} %get-tuple-element.12), channel_id=1, source_target_pairs={{0,8},{8,16},{16,24},{24,32},{32,40},{40,48},{48,56},{1,9},{9,17},... | collective-permute-start | bytes 92168 | tf_op jit(solution)/shard_map/ppermute | solution.py:21
  16.8 27.6 %collective-permute-start.1 = (f32[15,1,512]{2,1,0:T(1,128)S(1)}, f32[15,1,512]{2,1,0:T(1,128)S(1)}, u32[]{:S(2)}, u32[]{:S(2)}) collective-permute-start(f32[15,1,512]{2,1,0:T(1,128)S(1)} %get-tuple-element.13), channel_id=1, source_target_pairs={{8,0},{16,8},{24,16},{32,24},{40,32},{48,40},{56,48},{9,1},{17,9},... | collective-permute-start | bytes 92168 | tf_op jit(solution)/shard_map/ppermute | solution.py:24
  21.4 8.0 %collective-permute-start.6 = (f32[4,258,1]{1,0,2:T(4,128)S(1)}, f32[4,258,1]{1,0,2:T(4,128)S(1)}, u32[]{:S(2)}, u32[]{:S(2)}) collective-permute-start(f32[4,258,1]{1,0,2:T(4,128)S(1)} %copy.146), channel_id=1, source_target_pairs={{1,0},{2,1},{3,2},{4,3},{5,4},{6,5},{7,6},{9,8},{10,9},{11,10},{12... | collective-permute-start | bytes 12392 | tf_op jit(solution)/shard_map/ppermute | solution.py:24
  38.0 25.4 %collective-permute-start.7 = (f32[2,256,512]{2,1,0:T(8,128)}, f32[2,256,512]{2,1,0:T(8,128)S(1)}, u32[]{:S(2)}, u32[]{:S(2)}) collective-permute-start(f32[2,256,512]{2,1,0:T(8,128)} %maximum_select_fusion), channel_id=1, source_target_pairs={{0,64},{64,0},{1,65},{65,1},{2,66},{66,2},{3,67},{67,3},{4,68},{68... | collective-permute-start | bytes 3145736 | tf_op jit(solution)/shard_map/ppermute | solution.py:30
  42.1 27.4 %collective-permute-start.12 = (f32[4,258,1]{1,0,2:T(4,128)S(1)}, f32[4,258,1]{1,0,2:T(4,128)S(1)}, u32[]{:S(2)}, u32[]{:S(2)}) collective-permute-start(f32[4,258,1]{1,0,2:T(4,128)S(1)} %copy.149), channel_id=1, source_target_pairs={{0,1},{1,2},{2,3},{3,4},{4,5},{5,6},{6,7},{8,9},{9,10},{10,11},{11... | collective-permute-start | bytes 12392 | tf_op jit(solution)/shard_map/ppermute | solution.py:21
  51.3 19.3 %collective-permute-start.2 = (f32[15,258,1]{1,2,0:T(1,128)S(1)}, f32[15,258,1]{1,2,0:T(1,128)S(1)}, u32[]{:S(2)}, u32[]{:S(2)}) collective-permute-start(f32[15,258,1]{1,2,0:T(1,128)S(1)} %copy.138), channel_id=1, source_target_pairs={{0,1},{1,2},{2,3},{3,4},{4,5},{5,6},{6,7},{8,9},{9,10},{10,11},{11... | collective-permute-start | bytes 46448 | tf_op jit(solution)/shard_map/ppermute | solution.py:21
  55.7 16.9 %collective-permute-start.3 = (f32[15,258,1]{1,2,0:T(1,128)S(1)}, f32[15,258,1]{1,2,0:T(1,128)S(1)}, u32[]{:S(2)}, u32[]{:S(2)}) collective-permute-start(f32[15,258,1]{1,2,0:T(1,128)S(1)} %copy.139), channel_id=1, source_target_pairs={{1,0},{2,1},{3,2},{4,3},{5,4},{6,5},{7,6},{9,8},{10,9},{11,10},{12... | collective-permute-start | bytes 46448 | tf_op jit(solution)/shard_map/ppermute | solution.py:24
  63.4 11.2 %collective-permute-start.8 = (f32[2,1,512]{2,1,0:T(1,128)S(1)}, f32[2,1,512]{2,1,0:T(1,128)S(1)}, u32[]{:S(2)}, u32[]{:S(2)}) collective-permute-start(f32[2,1,512]{2,1,0:T(1,128)S(1)} %get-tuple-element.72), channel_id=1, source_target_pairs={{0,8},{8,16},{16,24},{24,32},{32,40},{40,48},{48,56},{1,9},{9,17},... | collective-permute-start | bytes 12296 | tf_op jit(solution)/shard_map/ppermute | solution.py:21
  67.6 7.1 %collective-permute-start.9 = (f32[2,1,512]{2,1,0:T(1,128)S(1)}, f32[2,1,512]{2,1,0:T(1,128)S(1)}, u32[]{:S(2)}, u32[]{:S(2)}) collective-permute-start(f32[2,1,512]{2,1,0:T(1,128)S(1)} %get-tuple-element.73), channel_id=1, source_target_pairs={{8,0},{16,8},{24,16},{32,24},{40,32},{48,40},{56,48},{9,1},{17,9},... | collective-permute-start | bytes 12296 | tf_op jit(solution)/shard_map/ppermute | solution.py:24
  74.8 20.6 %collective-permute-start.10 = (f32[2,258,1]{2,1,0:T(8,128)S(1)}, f32[2,258,1]{2,1,0:T(8,128)S(1)}, u32[]{:S(2)}, u32[]{:S(2)}) collective-permute-start(f32[2,258,1]{2,1,0:T(8,128)S(1)} %get-tuple-element.68), channel_id=1, source_target_pairs={{0,1},{1,2},{2,3},{3,4},{4,5},{5,6},{6,7},{8,9},{9,10},{10,11},{11... | collective-permute-start | bytes 6200 | tf_op jit(solution)/shard_map/ppermute | solution.py:21
  77.2 18.2 %collective-permute-start.11 = (f32[2,258,1]{2,1,0:T(8,128)S(1)}, f32[2,258,1]{2,1,0:T(8,128)S(1)}, u32[]{:S(2)}, u32[]{:S(2)}) collective-permute-start(f32[2,258,1]{2,1,0:T(8,128)S(1)} %get-tuple-element.69), channel_id=1, source_target_pairs={{1,0},{2,1},{3,2},{4,3},{5,4},{6,5},{7,6},{9,8},{10,9},{11,10},{12... | collective-permute-start | bytes 6200 | tf_op jit(solution)/shard_map/ppermute | solution.py:24
  129.1 14.6 %collective-permute-start.15 = (f32[4,258,1]{1,0,2:T(4,128)S(1)}, f32[4,258,1]{1,0,2:T(4,128)S(1)}, u32[]{:S(2)}, u32[]{:S(2)}) collective-permute-start(f32[4,258,1]{1,0,2:T(4,128)S(1)} %copy.156), channel_id=1, source_target_pairs={{1,0},{2,1},{3,2},{4,3},{5,4},{6,5},{7,6},{9,8},{10,9},{11,10},{12... | collective-permute-start | bytes 12392 | tf_op jit(solution)/shard_map/ppermute | solution.py:24
  132.3 12.4 %collective-permute-start.16 = (f32[4,258,1]{1,0,2:T(4,128)S(1)}, f32[4,258,1]{1,0,2:T(4,128)S(1)}, u32[]{:S(2)}, u32[]{:S(2)}) collective-permute-start(f32[4,258,1]{1,0,2:T(4,128)S(1)} %copy.158), channel_id=1, source_target_pairs={{0,1},{1,2},{2,3},{3,4},{4,5},{5,6},{6,7},{8,9},{9,10},{10,11},{11... | collective-permute-start | bytes 12392 | tf_op jit(solution)/shard_map/ppermute | solution.py:21
  167.9 14.4 %collective-permute-start.19 = (f32[4,258,1]{1,0,2:T(4,128)S(1)}, f32[4,258,1]{1,0,2:T(4,128)S(1)}, u32[]{:S(2)}, u32[]{:S(2)}) collective-permute-start(f32[4,258,1]{1,0,2:T(4,128)S(1)} %copy.166), channel_id=1, source_target_pairs={{1,0},{2,1},{3,2},{4,3},{5,4},{6,5},{7,6},{9,8},{10,9},{11,10},{12... | collective-permute-start | bytes 12392 | tf_op jit(solution)/shard_map/ppermute | solution.py:24
  171.1 12.2 %collective-permute-start.20 = (f32[4,258,1]{1,0,2:T(4,128)S(1)}, f32[4,258,1]{1,0,2:T(4,128)S(1)}, u32[]{:S(2)}, u32[]{:S(2)}) collective-permute-start(f32[4,258,1]{1,0,2:T(4,128)S(1)} %copy.168), channel_id=1, source_target_pairs={{0,1},{1,2},{2,3},{3,4},{4,5},{5,6},{6,7},{8,9},{9,10},{10,11},{11... | collective-permute-start | bytes 12392 | tf_op jit(solution)/shard_map/ppermute | solution.py:21
  206.5 14.8 %collective-permute-start.23 = (f32[4,258,1]{1,0,2:T(4,128)S(1)}, f32[4,258,1]{1,0,2:T(4,128)S(1)}, u32[]{:S(2)}, u32[]{:S(2)}) collective-permute-start(f32[4,258,1]{1,0,2:T(4,128)S(1)} %copy.176), channel_id=1, source_target_pairs={{1,0},{2,1},{3,2},{4,3},{5,4},{6,5},{7,6},{9,8},{10,9},{11,10},{12... | collective-permute-start | bytes 12392 | tf_op jit(solution)/shard_map/ppermute | solution.py:24
  209.7 12.6 %collective-permute-start.24 = (f32[4,258,1]{1,0,2:T(4,128)S(1)}, f32[4,258,1]{1,0,2:T(4,128)S(1)}, u32[]{:S(2)}, u32[]{:S(2)}) collective-permute-start(f32[4,258,1]{1,0,2:T(4,128)S(1)} %copy.178), channel_id=1, source_target_pairs={{0,1},{1,2},{2,3},{3,4},{4,5},{5,6},{6,7},{8,9},{9,10},{10,11},{11... | collective-permute-start | bytes 12392 | tf_op jit(solution)/shard_map/ppermute | solution.py:21
  244.3 8.0 %collective-permute-start.27 = (f32[4,258,1]{1,0,2:T(4,128)S(1)}, f32[4,258,1]{1,0,2:T(4,128)S(1)}, u32[]{:S(2)}, u32[]{:S(2)}) collective-permute-start(f32[4,258,1]{1,0,2:T(4,128)S(1)} %copy.186), channel_id=1, source_target_pairs={{1,0},{2,1},{3,2},{4,3},{5,4},{6,5},{7,6},{9,8},{10,9},{11,10},{12... | collective-permute-start | bytes 12392 | tf_op jit(solution)/shard_map/ppermute | solution.py:24
  259.9 24.7 %collective-permute-start.28 = (f32[2,256,512]{2,1,0:T(8,128)S(1)}, f32[2,256,512]{2,1,0:T(8,128)S(1)}, u32[]{:S(2)}, u32[]{:S(2)}) collective-permute-start(f32[2,256,512]{2,1,0:T(8,128)S(1)} %slice_select_fusion), channel_id=1, source_target_pairs={{0,64},{64,0},{1,65},{65,1},{2,66},{66,2},{3,67},{67,3},{4,68},{68... | collective-permute-start | bytes 3145736 | tf_op jit(solution)/shard_map/ppermute | solution.py:30
  284.6 9.3 %collective-permute-start.29 = (f32[2,1,512]{2,1,0:T(1,128)S(1)}, f32[2,1,512]{2,1,0:T(1,128)S(1)}, u32[]{:S(2)}, u32[]{:S(2)}) collective-permute-start(f32[2,1,512]{2,1,0:T(1,128)S(1)} %get-tuple-element.70), channel_id=1, source_target_pairs={{0,8},{8,16},{16,24},{24,32},{32,40},{40,48},{48,56},{1,9},{9,17},... | collective-permute-start | bytes 12296 | tf_op jit(solution)/shard_map/ppermute | solution.py:21
  292.0 12.4 %collective-permute-start.33 = (f32[4,258,1]{1,0,2:T(4,128)S(1)}, f32[4,258,1]{1,0,2:T(4,128)S(1)}, u32[]{:S(2)}, u32[]{:S(2)}) collective-permute-start(f32[4,258,1]{1,0,2:T(4,128)S(1)} %copy.189), channel_id=1, source_target_pairs={{0,1},{1,2},{2,3},{3,4},{4,5},{5,6},{6,7},{8,9},{9,10},{10,11},{11... | collective-permute-start | bytes 12392 | tf_op jit(solution)/shard_map/ppermute | solution.py:21
  294.8 10.6 %collective-permute-start.31 = (f32[2,258,1]{2,1,0:T(8,128)}, f32[2,258,1]{2,1,0:T(8,128)S(1)}, u32[]{:S(2)}, u32[]{:S(2)}) collective-permute-start(f32[2,258,1]{2,1,0:T(8,128)} %get-tuple-element.66), channel_id=1, source_target_pairs={{0,1},{1,2},{2,3},{3,4},{4,5},{5,6},{6,7},{8,9},{9,10},{10,11},{11... | collective-permute-start | bytes 6200 | tf_op jit(solution)/shard_map/ppermute | solution.py:21
  296.7 12.4 %collective-permute-start.32 = (f32[2,258,1]{2,1,0:T(8,128)}, f32[2,258,1]{2,1,0:T(8,128)}, u32[]{:S(2)}, u32[]{:S(2)}) collective-permute-start(f32[2,258,1]{2,1,0:T(8,128)} %get-tuple-element.67), channel_id=1, source_target_pairs={{1,0},{2,1},{3,2},{4,3},{5,4},{6,5},{7,6},{9,8},{10,9},{11,10},{12... | collective-permute-start | bytes 6200 | tf_op jit(solution)/shard_map/ppermute | solution.py:24
  330.9 6.4 %collective-permute-start.34 = (f32[4,1,512]{2,0,1:T(4,128)S(1)}, f32[4,1,512]{2,0,1:T(4,128)S(1)}, u32[]{:S(2)}, u32[]{:S(2)}) collective-permute-start(f32[4,1,512]{2,0,1:T(4,128)S(1)} %copy.192), channel_id=1, source_target_pairs={{0,8},{8,16},{16,24},{24,32},{32,40},{40,48},{48,56},{1,9},{9,17},... | collective-permute-start | bytes 24584 | tf_op jit(solution)/shard_map/ppermute | solution.py:21
  342.9 14.4 %collective-permute-start.36 = (f32[4,258,1]{1,0,2:T(4,128)S(1)}, f32[4,258,1]{1,0,2:T(4,128)S(1)}, u32[]{:S(2)}, u32[]{:S(2)}) collective-permute-start(f32[4,258,1]{1,0,2:T(4,128)S(1)} %copy.196), channel_id=1, source_target_pairs={{1,0},{2,1},{3,2},{4,3},{5,4},{6,5},{7,6},{9,8},{10,9},{11,10},{12... | collective-permute-start | bytes 12392 | tf_op jit(solution)/shard_map/ppermute | solution.py:24
  346.1 12.2 %collective-permute-start.37 = (f32[4,258,1]{1,0,2:T(4,128)S(1)}, f32[4,258,1]{1,0,2:T(4,128)S(1)}, u32[]{:S(2)}, u32[]{:S(2)}) collective-permute-start(f32[4,258,1]{1,0,2:T(4,128)S(1)} %copy.198), channel_id=1, source_target_pairs={{0,1},{1,2},{2,3},{3,4},{4,5},{5,6},{6,7},{8,9},{9,10},{10,11},{11... | collective-permute-start | bytes 12392 | tf_op jit(solution)/shard_map/ppermute | solution.py:21
  381.8 14.6 %collective-permute-start.40 = (f32[4,258,1]{1,0,2:T(4,128)S(1)}, f32[4,258,1]{1,0,2:T(4,128)S(1)}, u32[]{:S(2)}, u32[]{:S(2)}) collective-permute-start(f32[4,258,1]{1,0,2:T(4,128)S(1)} %copy.206), channel_id=1, source_target_pairs={{1,0},{2,1},{3,2},{4,3},{5,4},{6,5},{7,6},{9,8},{10,9},{11,10},{12... | collective-permute-start | bytes 12392 | tf_op jit(solution)/shard_map/ppermute | solution.py:24
  385.0 12.4 %collective-permute-start.41 = (f32[4,258,1]{1,0,2:T(4,128)S(1)}, f32[4,258,1]{1,0,2:T(4,128)S(1)}, u32[]{:S(2)}, u32[]{:S(2)}) collective-permute-start(f32[4,258,1]{1,0,2:T(4,128)S(1)} %copy.208), channel_id=1, source_target_pairs={{0,1},{1,2},{2,3},{3,4},{4,5},{5,6},{6,7},{8,9},{9,10},{10,11},{11... | collective-permute-start | bytes 12392 | tf_op jit(solution)/shard_map/ppermute | solution.py:21
  420.9 14.4 %collective-permute-start.44 = (f32[4,258,1]{1,0,2:T(4,128)S(1)}, f32[4,258,1]{1,0,2:T(4,128)S(1)}, u32[]{:S(2)}, u32[]{:S(2)}) collective-permute-start(f32[4,258,1]{1,0,2:T(4,128)S(1)} %copy.216), channel_id=1, source_target_pairs={{1,0},{2,1},{3,2},{4,3},{5,4},{6,5},{7,6},{9,8},{10,9},{11,10},{12... | collective-permute-start | bytes 12392 | tf_op jit(solution)/shard_map/ppermute | solution.py:24
  424.1 12.3 %collective-permute-start.45 = (f32[4,258,1]{1,0,2:T(4,128)S(1)}, f32[4,258,1]{1,0,2:T(4,128)S(1)}, u32[]{:S(2)}, u32[]{:S(2)}) collective-permute-start(f32[4,258,1]{1,0,2:T(4,128)S(1)} %copy.218), channel_id=1, source_target_pairs={{0,1},{1,2},{2,3},{3,4},{4,5},{5,6},{6,7},{8,9},{9,10},{10,11},{11... | collective-permute-start | bytes 12392 | tf_op jit(solution)/shard_map/ppermute | solution.py:21
  (51 other events, 303.9 us)
where the time goes:
time: 459 us; the launch traced here: 451 us
  other arithmetic  152 us (33%)
  starting transfers between devices  139 us (30%)
  local copies, waits for them, and re-layouts  94.4 us (21%)
  waiting for transfers between devices  64.1 us (14%)
    ppermute x22, starting transfers between devices, with_halo(): lax.ppermute(lax.slice_in_dim(block, block.shape[dim] - width, None, axis...  90.3 us
    mul x8, other arithmetic, relax(): current = current * trim_rim(inside_mask, 1)  76.9 us
    ppermute x22, starting transfers between devices, with_halo(): lax.ppermute(lax.slice_in_dim(block, 0, width, axis=dim), axis, backward)  47.1 us
    ppermute x22, waiting for transfers between devices, with_halo(): lax.ppermute(lax.slice_in_dim(block, 0, width, axis=dim), axis, backward)  35.6 us
    slice x8, local copies, waits for them, and re-layouts, sweep_once(): above = jnp.concatenate([zero_plane, center[:-1]], 0)  31.1 us
    ppermute x2, waiting for transfers between devices, from_partner(): lax.ppermute(shard, axis, [(i, i ^ 1 << distance) for i in range(lax.axis...  28.4 us
    concatenate x3, other arithmetic, with_halo(): block = jnp.concatenate([low, block, high], axis=dim)  17.4 us
    broadcast_in_dim x1, other arithmetic, shards(): return state[None]  13.2 us
  transfers between devices with their start and end apart: 46, of which 12 were waited for; matrix products, arithmetic and copies ran while one was open for 21% of the time, Pallas kernels for 0%

commit v1 on v0

v1 whole, which is shorter than its diff:
```python
import functools

import jax
import jax.numpy as jnp
from jax import lax
from jax.experimental import pallas as pl
from jax.experimental.pallas import tpu as pltpu
from jax.sharding import PartitionSpec as P

MESH = pl.DeviceIdType.MESH
F32 = jnp.float32
SWEEPS = 4
STEPS = 2
LEAK = 0.05
TEMP_COEF = 0.5

LANES = 128
HALO = 8
GUARD = 8
R = 16
STRIP = 8
PACKED = 16


def kernel(
    grid_rows, grid_cols,
    state_in, cx_in, cy_in, act_in, class_in, table, via_in, out,
    x, y, z, cx, cy, ce, cs, rw, ky, vert, load, src, act, cls, via,
    send_map, recv_map, pack_send, pack_recv,
    load_sem, row_send_sem, row_recv_sem, col_send_sem, col_recv_sem,
    map_send_sem, map_recv_sem, out_sem,
):
    rows, cols = state_in.shape[2], state_in.shape[3]
    tiles = cols // LANES
    wide = rows + 2 * HALO
    chunks = wide // R
    field = lax.axis_index("field")
    row = lax.axis_index("row")
    col = lax.axis_index("col")
    is_elec = field == 0
    has_n, has_s = row > 0, row < grid_rows - 1
    has_w, has_e = col > 0, col < grid_cols - 1
    lane = lax.broadcasted_iota(jnp.int32, (1, LANES), 1)
    lane3 = lax.broadcasted_iota(jnp.int32, (1, 1, LANES), 2)
    arrays = (
        (state_in, x, GUARD), (cx_in, cx, GUARD), (cy_in, cy, GUARD),
        (via_in, via, 0), (act_in, act, 0), (class_in, cls, 0),
    )

    def lanes_of(t):
        return pl.ds(pl.multiple_of(t * LANES, LANES), LANES)

    def pick(item, first, dest, count, t):
        source, target, base = item
        spot = pl.ds(base + dest, count)
        if len(source.shape) == 4:
            return source.at[0, :, pl.ds(first, count), lanes_of(t)], target.at[:, t, spot, :]
        return source.at[0, pl.ds(first, count), lanes_of(t)], target.at[t, spot, :]

    def local_copy(k, t):
        a, b = pick(arrays[k], 0, HALO, rows, t)
        return pltpu.make_async_copy(a, b, load_sem.at[k, t])

    def row_copy(k, t, down):
        first, dest = (rows - HALO, 0) if down else (0, rows + HALO)
        a, b = pick(arrays[k], first, dest, HALO, t)
        return pltpu.make_async_remote_copy(
            src_ref=a, dst_ref=b,
            send_sem=row_send_sem.at[int(down), k, t], recv_sem=row_recv_sem.at[int(down), k, t],
            device_id={"row": row + 1 if down else row - 1}, device_id_type=MESH,
        )

    def each_tile(action):
        def body(t, carry):
            for k in range(len(arrays)):
                action(k, t)
            return carry
        lax.fori_loop(0, tiles, body, 0)

    each_tile(lambda k, t: local_copy(k, t).start())

    barrier = pltpu.get_barrier_semaphore()
    pl.semaphore_signal(barrier, inc=1, device_id={"field": 1 - field}, device_id_type=MESH)
    for dr, has_r in ((-1, has_n), (0, None), (1, has_s)):
        for dc, has_c in ((-1, has_w), (0, None), (1, has_e)):
            if dr == 0 and dc == 0:
                continue
            there = has_c if has_r is None else has_r if has_c is None else has_r & has_c

            @pl.when(there)
            def _(dr=dr, dc=dc):
                pl.semaphore_signal(
                    barrier, inc=1, device_id={"row": row + dr, "col": col + dc}, device_id_type=MESH
                )
    near_r = 1 + has_n.astype(jnp.int32) + has_s.astype(jnp.int32)
    near_c = 1 + has_w.astype(jnp.int32) + has_e.astype(jnp.int32)
    pl.semaphore_wait(barrier, near_r * near_c)

    @pl.when(has_n)
    def _():
        each_tile(lambda k, t: row_copy(k, t, False).start())

    @pl.when(has_s)
    def _():
        each_tile(lambda k, t: row_copy(k, t, True).start())

    def clear_rows(dest):
        for source, target, base in arrays:
            spot = pl.ds(base + dest, HALO)
            if len(source.shape) == 4:
                target[:, 0:tiles, spot, :] = jnp.zeros(
                    (target.shape[0], tiles, HALO, LANES), target.dtype)
            else:
                target[:, spot, :] = jnp.zeros((tiles, HALO, LANES), target.dtype)

    @pl.when(jnp.logical_not(has_n))
    def _():
        clear_rows(0)

    @pl.when(jnp.logical_not(has_s))
    def _():
        clear_rows(rows + HALO)

    def prepare(first, count, t):
        spot = pl.ds(first, count)
        spot_g = pl.ds(first + GUARD, count)
        ids = cls[t, spot, :]
        density = jnp.where(ids == 1, table[0, 1], table[0, 0])
        for k in range(2, table.shape[1]):
            density = jnp.where(ids == k, table[0, k], density)
        load[t, spot_g, :] = density * act[t, spot, :]
        for q in range(3):
            vert[q, t, spot_g, :] = via[q, t, spot, :].astype(F32)

    each_tile(lambda k, t: local_copy(k, t).wait())

    def prepare_tile(t, carry):
        def body(i, carry):
            prepare(pl.multiple_of(HALO + i * 32, 8), 32, t)
            return carry
        return lax.fori_loop(0, rows // 32, body, carry)
    lax.fori_loop(0, tiles, prepare_tile, 0)

    def plane_at(q, t, spot):
        if q < 4:
            return x, (q, t, spot, slice(None))
        if q < 8:
            return cx, (q - 4, t, spot, slice(None))
        if q < 12:
            return cy, (q - 8, t, spot, slice(None))
        if q == 12:
            return load, (t, spot, slice(None))
        return vert, (q - 13, t, spot, slice(None))

    group = lane // 8

    def pack(i, carry):
        first = pl.multiple_of(i * 32, 32)
        spot = pl.ds(first + GUARD + HALO, 32)
        west = jnp.zeros((32, LANES), F32)
        east = jnp.zeros((32, LANES), F32)
        for q in range(PACKED):
            ref, index = plane_at(q, 0, spot)
            west = jnp.where(group == q, pltpu.roll(ref[index], 8 * q, 1) if q else ref[index], west)
            ref, index = plane_at(q, tiles - 1, spot)
            shift = (8 * q + 8) % LANES
            east = jnp.where(group == q, pltpu.roll(ref[index], shift, 1) if shift else ref[index], east)
        pack_send[0, pl.ds(first, 32), :] = west
        pack_send[1, pl.ds(first, 32), :] = east
        return carry
    lax.fori_loop(0, rows // 32, pack, 0)

    def col_copy(side, dr):
        first, dest, count = ((0, rows + HALO, HALO), (0, HALO, rows), (rows - HALO, 0, HALO))[dr + 1]
        return pltpu.make_async_remote_copy(
            src_ref=pack_send.at[side, pl.ds(first, count), :],
            dst_ref=pack_recv.at[side, pl.ds(dest, count), :],
            send_sem=col_send_sem.at[side, dr + 1], recv_sem=col_recv_sem.at[side, dr + 1],
            device_id={"row": row + dr, "col": col + (1 if side else -1)}, device_id_type=MESH,
        )

    def each_side(action, incoming):
        for side in range(2):
            for dr in (0, -1, 1):
                has_c = (has_w, has_e)[1 - side if incoming else side]
                step = -dr if incoming else dr
                there = has_c if step == 0 else has_c & (has_n if step < 0 else has_s)
                action(side, dr, there)

    def send_side(side, dr, there):
        @pl.when(there)
        def _():
            col_copy(side, dr).start()

    each_side(send_side, False)

    @pl.when(has_s)
    def _():
        each_tile(lambda k, t: row_copy(k, t, False).wait_recv())

    @pl.when(has_n)
    def _():
        each_tile(lambda k, t: row_copy(k, t, True).wait_recv())

    def prepare_edge(t, carry):
        prepare(0, HALO, t)
        prepare(rows + HALO, HALO, t)
        return carry
    lax.fori_loop(0, tiles, prepare_edge, 0)

    def recv_side(side, dr, there):
        _, dest, count = ((0, rows + HALO, HALO), (0, HALO, rows), (0, 0, HALO))[dr + 1]

        @pl.when(there)
        def _():
            col_copy(side, dr).wait_recv()

        @pl.when(jnp.logical_not(there))
        def _():
            pack_recv[side, pl.ds(dest, count), :] = jnp.zeros((count, LANES), F32)

    each_side(recv_side, True)

    def unpack(c, carry):
        first = pl.multiple_of(c * R, R)
        spot = pl.ds(first + GUARD, R)
        east = pack_recv[0, pl.ds(first, R), :]
        west = pack_recv[1, pl.ds(first, R), :]
        for q in range(PACKED):
            e = pltpu.roll(east, LANES - 8 * q, 1) if q else east
            shift = (120 - 8 * q) % LANES
            w = pltpu.roll(west, shift, 1) if shift else west
            ref, index = plane_at(q, tiles, spot)
            ref[index] = jnp.where(lane < 64, e, w)
        return carry
    lax.fori_loop(0, chunks, unpack, 0)

    def from_east(v):
        r = pltpu.roll(v, LANES - 1, 2)
        return jnp.where(lane3 == LANES - 1, jnp.concatenate([r[1:], r[:1]], 0), r)

    def from_west(v):
        r = pltpu.roll(v, 1, 2)
        return jnp.where(lane3 == 0, jnp.concatenate([r[-1:], r[:-1]], 0), r)

    def at(first):
        return pl.ds(first + GUARD, R)

    def half_east():
        tile = lax.broadcasted_iota(jnp.int32, (tiles + 1, 1, LANES), 0)
        closed = (lane3 == LANES - 1) & (
            ((tile == tiles - 1) & jnp.logical_not(has_e)) | ((tile == tiles) & jnp.logical_not(has_w)))
        return jnp.where(closed, 0.0, 0.5).astype(F32)

    def half_south(first):
        at_row = first + lax.broadcasted_iota(jnp.int32, (1, R, LANES), 1)
        closed = ((at_row == HALO - 1) & jnp.logical_not(has_n)) | (
            (at_row == HALO + rows - 1) & jnp.logical_not(has_s))
        return jnp.where(closed, 0.0, 0.5).astype(F32)

    def links_of(p, elec, first):
        if elec:
            return vert[0 if p < 2 else 2, :, at(first), :]
        if p == 0:
            return vert[0, :, at(first), :]
        if p == 3:
            return vert[2, :, at(first), :]
        return vert[p - 1, :, at(first), :] + vert[p, :, at(first), :]

    def face_rows(first, elec):
        kappa = ky if elec else cy
        here, above = half_south(first), half_south(first - 1)
        for p in range(4):
            k = kappa[p, :, at(first), :]
            south = here * (k + kappa[p, :, at(first + 1), :])
            north = above * (k + kappa[p, :, at(first - 1), :])
            east = ce[p, :, at(first), :]
            cs[p, :, at(first), :] = south
            weight = east + from_west(east) + south + north + links_of(p, elec, first) + LEAK
            rw[p, :, at(first), :] = 1.0 / weight

    def sweep(old, new, first, elec):
        for p in range(4):
            v = old[p, :, at(first), :]
            east = ce[p, :, at(first), :]
            total = east * from_east(v) + from_west(east * v)
            total = total + cs[p, :, at(first), :] * old[p, :, at(first + 1), :]
            total = total + cs[p, :, at(first - 1), :] * old[p, :, at(first - 1), :]
            if elec:
                total = total + vert[0 if p < 2 else 2, :, at(first), :] * old[p ^ 1, :, at(first), :]
                if p in (1, 2):
                    total = total + load[:, at(first), :]
            else:
                if p > 0:
                    total = total + vert[p - 1, :, at(first), :] * old[p - 1, :, at(first), :]
                if p < 3:
                    total = total + vert[p, :, at(first), :] * old[p + 1, :, at(first), :]
                if p < 2:
                    total = total + src[p, :, at(first), :]
            new[p, :, at(first), :] = total * rw[p, :, at(first), :]

    strip_group = lane // 16

    def write_map(step, c, planes):
        strip = jnp.zeros((STRIP, LANES), F32)
        for q in range(2):
            send_map[step, c, pl.ds(q * tiles * R, tiles * R), :] = planes[q][:tiles].reshape(tiles * R, LANES)
            for b in range(R // 8):
                k = 2 * b + q
                strip = jnp.where(
                    strip_group == k, pltpu.roll(planes[q][tiles, 8 * b : 8 * b + 8], 8 + 16 * k, 1), strip)
        send_map[step, c, pl.ds(2 * tiles * R, STRIP), :] = strip

    def read_map(step, c):
        strip = recv_map[step, c, pl.ds(2 * tiles * R, STRIP), :]
        planes = []
        for q in range(2):
            main = recv_map[step, c, pl.ds(q * tiles * R, tiles * R), :].reshape(tiles, R, LANES)
            parts = [pltpu.roll(strip, LANES - (8 + 16 * (2 * b + q)), 1) for b in range(R // 8)]
            planes.append(jnp.concatenate([main, jnp.concatenate(parts, 0)[None]], 0))
        return planes

    def map_copy(step, c):
        return pltpu.make_async_remote_copy(
            src_ref=send_map.at[step, c], dst_ref=recv_map.at[step, c],
            send_sem=map_send_sem.at[step, c], recv_sem=map_recv_sem.at[step, c],
            device_id={"field": 1 - field}, device_id_type=MESH,
        )

    def send_chunk(step, c, state):
        first = pl.multiple_of(c * R, R)

        @pl.when(is_elec)
        def _():
            heats = []
            for p in range(4):
                v = state[p, :, at(first), :]
                de = v - from_east(v)
                ds = v - state[p, :, at(first + 1), :]
                heats.append(cx[p, :, at(first), :] * (de * de) + cy[p, :, at(first), :] * (ds * ds))
            write_map(step, c, (heats[0] + heats[3], heats[1] + heats[2]))

        @pl.when(jnp.logical_not(is_elec))
        def _():
            write_map(step, c, (state[0, :, at(first), :], state[1, :, at(first), :]))

        map_copy(step, c).start()

    def first_maps(c, carry):
        send_chunk(0, c, x)
        return carry
    lax.fori_loop(0, chunks, first_maps, 0)

    @pl.when(jnp.logical_not(is_elec))
    def _():
        def body(c, carry):
            first = pl.multiple_of(c * R, R)
            he = half_east()
            for p in range(4):
                k = cx[p, :, at(first), :]
                ce[p, :, at(first), :] = he * (k + from_east(k))
            face_rows(first - 1, False)
            return carry
        lax.fori_loop(0, chunks, body, 0)

    def advance(step, c, buffers):
        first = pl.multiple_of(c * R, R)
        map_copy(step, c).wait_recv()

        @pl.when(is_elec)
        def _():
            temps = read_map(step, c)
            factor = [1.0 / (1.0 + TEMP_COEF * t) for t in temps]
            he = half_east()
            for p in range(4):
                f = factor[(0, 1, 1, 0)[p]]
                k = cx[p, :, at(first), :] * f
                ce[p, :, at(first), :] = he * (k + from_east(k))
                ky[p, :, at(first), :] = cy[p, :, at(first), :] * f
            face_rows(first - 1, True)
            for s in range(SWEEPS):
                sweep(buffers[s], buffers[s + 1], first - 1 - s, True)

        @pl.when(jnp.logical_not(is_elec))
        def _():
            joule = read_map(step, c)
            src[0, :, at(first), :] = joule[0]
            src[1, :, at(first), :] = joule[1] + load[:, at(first), :]
            for s in range(SWEEPS):
                sweep(buffers[s], buffers[s + 1], first - 1 - s, False)

    def step_one(c, carry):
        @pl.when(c < chunks)
        def _():
            advance(0, c, (x, y, z, y, z))

        @pl.when(c > 0)
        def _():
            send_chunk(1, c - 1, z)
        return carry
    lax.fori_loop(0, chunks + 1, step_one, 0)

    def out_copy(c, t):
        return pltpu.make_async_copy(
            x.at[:, t, pl.ds(pl.multiple_of(c * R + GUARD + HALO, 8), R), :],
            out.at[0, :, pl.ds(pl.multiple_of(c * R, R), R), lanes_of(t)],
            out_sem.at[c, t],
        )

    def step_two(c, carry):
        advance(1, c, (z, y, x, y, x))

        @pl.when(c > 0)
        def _():
            for t in range(tiles):
                out_copy(c - 1, t).start()
        return carry
    lax.fori_loop(0, chunks, step_two, 0)

    def finish(c, carry):
        for step in range(STEPS):
            map_copy(step, c).wait_send()

        @pl.when(c > 0)
        def _():
            for t in range(tiles):
                out_copy(c - 1, t).wait()
        return carry
    lax.fori_loop(0, chunks, finish, 0)

    @pl.when(has_n)
    def _():
        each_tile(lambda k, t: row_copy(k, t, False).wait_send())

    @pl.when(has_s)
    def _():
        each_tile(lambda k, t: row_copy(k, t, True).wait_send())

    def sent_side(side, dr, there):
        @pl.when(there)
        def _():
            col_copy(side, dr).wait_send()

    each_side(sent_side, False)


def shards(grid_rows, grid_cols, *args):
    rows, cols = args[0].shape[2], args[0].shape[3]
    tiles = cols // LANES
    wide = rows + 2 * HALO
    chunks = wide // R
    tall = wide + 2 * GUARD
    field = pltpu.VMEM((4, tiles + 1, tall, LANES), F32)
    message = 2 * tiles * R + STRIP
    dma = pltpu.SemaphoreType.DMA
    hbm = pl.BlockSpec(memory_space=pl.ANY)
    return pl.pallas_call(
        functools.partial(kernel, grid_rows, grid_cols),
        name="coupled_sweeps",
        out_shape=jax.ShapeDtypeStruct(args[0].shape, F32),
        in_specs=[hbm] * 5 + [pl.BlockSpec(memory_space=pltpu.SMEM), hbm],
        out_specs=hbm,
        scratch_shapes=[
            *[field] * 9,
            pltpu.VMEM((3, tiles + 1, tall, LANES), F32),
            pltpu.VMEM((tiles + 1, tall, LANES), F32),
            pltpu.VMEM((2, tiles + 1, tall, LANES), F32),
            pltpu.VMEM((tiles, wide, LANES), F32),
            pltpu.VMEM((tiles, wide, LANES), jnp.int32),
            pltpu.VMEM((3, tiles, wide, LANES), jnp.int32),
            pltpu.VMEM((STEPS, chunks, message, LANES), F32),
            pltpu.VMEM((STEPS, chunks, message, LANES), F32),
            pltpu.VMEM((2, rows, LANES), F32),
            pltpu.VMEM((2, wide, LANES), F32),
            dma((6, tiles)), dma((2, 6, tiles)), dma((2, 6, tiles)), dma((2, 3)), dma((2, 3)),
            dma((STEPS, chunks)), dma((STEPS, chunks)), dma((chunks, tiles)),
        ],
        compiler_params=pltpu.CompilerParams(
            collective_id=0, has_side_effects=True, vmem_limit_bytes=60 * 1024 * 1024
        ),
    )(*args)


def solution(mesh):
    return jax.shard_map(
        functools.partial(shards, mesh.shape["row"], mesh.shape["col"]),
        mesh=mesh,
        in_specs=(
            P("field", None, "row", "col"),
            P("field", None, "row", "col"),
            P("field", None, "row", "col"),
            P("field", "row", "col"),
            P("field", "row", "col"),
            P("field", None),
            P("field", None, "row", "col"),
        ),
        out_specs=P("field", None, "row", "col"),
        check_vma=False,
    )
```

time: 459 us -> 77.3 us (0.17); the launches traced: 451 us -> 76.4 us
  other arithmetic: 152 us -> 0 us
  starting transfers between devices: 139 us -> 0 us
  local copies, waits for them, and re-layouts: 94.4 us -> 3.08 us
  Pallas kernels: 0 us -> 73.3 us
  waiting for transfers between devices: 64.1 us -> 0 us
    ppermute x46 -> x0, starting transfers between devices: 139 us -> none  [the longest x22 90.3 us: with_halo(): lax.ppermute(lax.slice_in_dim(block, block.shape[dim] - width, None, axis...]
    mul x18 -> x0, other arithmetic: 91.4 us -> none  [the longest x8 76.9 us: relax(): current = current * trim_rim(inside_mask, 1)]
    pallas_call x0 -> x1, Pallas kernels: none -> 73.3 us  [shards(): pl.pallas_call(functools.partial(kernel, grid_rows, grid_cols), name='cou...]
    ppermute x46 -> x0, waiting for transfers between devices: 64.1 us -> none  [the longest x22 35.6 us: with_halo(): lax.ppermute(lax.slice_in_dim(block, 0, width, axis=dim), axis, backward)]
    slice x58 -> x0, local copies, waits for them, and re-layouts: 59.3 us -> none  [the longest x8 31.1 us: sweep_once(): above = jnp.concatenate([zero_plane, center[:-1]], 0)]
    ppermute x34 -> x0, local copies, waits for them, and re-layouts: 19.5 us -> none  [the longest x17 10.5 us: with_halo(): lax.ppermute(lax.slice_in_dim(block, block.shape[dim] - width, None, axis...]
    concatenate x3 -> x0, other arithmetic: 17.4 us -> none  [with_halo(): block = jnp.concatenate([low, block, high], axis=dim)]
    slice x12 -> x0, other arithmetic: 16 us -> none  [the longest x8 10.4 us: with_halo(): lax.slice_in_dim(block, 0, width, axis=dim)]
  transfers between devices with their start and end apart: 46 -> 0, of which waited for: 12 -> 0; matrix products, arithmetic and copies ran while one was open for 21% -> 0% of each run, Pallas kernels for 0% -> 0%
where the time goes in v1:
time: 77.3 us; the launch traced here: 76.4 us
  Pallas kernels  73.3 us (95%)
  local copies, waits for them, and re-layouts  3.08 us (4%)
    pallas_call x1, Pallas kernels, shards(): pl.pallas_call(functools.partial(kernel, grid_rows, grid_cols), name='cou...  73.3 us
    unnamed x1, local copies, waits for them, and re-layouts  3.08 us

profile of v1, /device:TPU:25, one launch (start us, length us, event | category | flops | bytes accessed | tf_op | source)
XLA Modules:
  0.0 76.4 jit_solution(16292159052271217980)
XLA Ops:
  0.0 73.3 %coupled_sweeps.1 = f32[1,4,256,512]{3,2,1,0:T(8,128)} custom-call(f32[1,4,256,512]{3,2,1,0:T(8,128)} %state_in.1, f32[1,4,256,512]{3,2,1,0:T(8,128)} %cx_in.1, f32[1,4,256,512]{3,2,1,0:T(8,128)} %cy_in.1, f32[1,256,512]{2,1,0:T(8,128)} %act_in.1, s32[1,256,512]{2,1,0:T(8,128)} %class_in.1, f32[1,8]{1,0:T(1,128)} %table.1, s32[1,3,256,512]{3,2,1,0:T(8,128)} %via_in.1), custom_call_target="tpu_custom_call" | custom-call | tf_op jit(solution)/shard_map/coupled_sweeps/pallas_call | solution.py:457
  73.3 3.1 %copy.9 = f32[1,4,256,512]{3,2,1,0:T(8,128)} copy(f32[1,4,256,512]{3,2,1,0:T(8,128)} %coupled_sweeps.1) | data formatting | bytes 4194304

commit v2 on v1

--- a/solution.py
+++ b/solution.py
@@ -10,7 +10,6 @@
 MESH = pl.DeviceIdType.MESH
 F32 = jnp.float32
 SWEEPS = 4
-STEPS = 2
 LEAK = 0.05
 TEMP_COEF = 0.5
 
@@ -18,7 +17,8 @@
 HALO = 8
 GUARD = 8
 R = 16
-STRIP = 8
+STRIP = 4
+EARLY = 6
 PACKED = 16
 
 
@@ -26,9 +26,9 @@
     grid_rows, grid_cols,
     state_in, cx_in, cy_in, act_in, class_in, table, via_in, out,
     x, y, z, cx, cy, ce, cs, rw, ky, vert, load, src, act, cls, via,
-    send_map, recv_map, pack_send, pack_recv,
+    send_main, recv_main, send_strip, recv_strip, send_map, recv_map, pack_send, pack_recv,
     load_sem, row_send_sem, row_recv_sem, col_send_sem, col_recv_sem,
-    map_send_sem, map_recv_sem, out_sem,
+    main_send_sem, main_recv_sem, strip_sem, map_send_sem, map_recv_sem, out_sem,
 ):
     rows, cols = state_in.shape[2], state_in.shape[3]
     tiles = cols // LANES
@@ -59,14 +59,32 @@
 
     def local_copy(k, t):
         a, b = pick(arrays[k], 0, HALO, rows, t)
-        return pltpu.make_async_copy(a, b, load_sem.at[k, t])
+        return pltpu.make_async_copy(a, b, load_sem.at[k])
+
+    def whole(k, dest, count):
+        source, target, base = arrays[k]
+        spot = pl.ds(base + dest, count)
+        if len(source.shape) == 4:
+            return target.at[:, pl.ds(0, tiles), spot, :]
+        return target.at[:, spot, :]
+
+    def wait_for(ref, sem):
+        pltpu.make_async_copy(ref, ref, sem).wait()
+
+    def loaded(*ks):
+        for k in ks:
+            wait_for(whole(k, HALO, rows), load_sem.at[k])
+
+    def rows_done(sem, down):
+        for k in range(len(arrays)):
+            wait_for(whole(k, 0 if down else rows + HALO, HALO), sem.at[int(down), k])
 
     def row_copy(k, t, down):
         first, dest = (rows - HALO, 0) if down else (0, rows + HALO)
         a, b = pick(arrays[k], first, dest, HALO, t)
         return pltpu.make_async_remote_copy(
             src_ref=a, dst_ref=b,
-            send_sem=row_send_sem.at[int(down), k, t], recv_sem=row_recv_sem.at[int(down), k, t],
+            send_sem=row_send_sem.at[int(down), k], recv_sem=row_recv_sem.at[int(down), k],
             device_id={"row": row + 1 if down else row - 1}, device_id_type=MESH,
         )
 
@@ -77,7 +95,12 @@
             return carry
         lax.fori_loop(0, tiles, body, 0)
 
-    each_tile(lambda k, t: local_copy(k, t).start())
+    def load_tiles(t, carry, ks):
+        for k in ks:
+            local_copy(k, t).start()
+        return carry
+    for ks in ((0, 1, 2), (3, 4, 5)):
+        lax.fori_loop(0, tiles, functools.partial(load_tiles, ks=ks), 0)
 
     barrier = pltpu.get_barrier_semaphore()
     pl.semaphore_signal(barrier, inc=1, device_id={"field": 1 - field}, device_id_type=MESH)
@@ -92,18 +115,6 @@
                 pl.semaphore_signal(
                     barrier, inc=1, device_id={"row": row + dr, "col": col + dc}, device_id_type=MESH
                 )
-    near_r = 1 + has_n.astype(jnp.int32) + has_s.astype(jnp.int32)
-    near_c = 1 + has_w.astype(jnp.int32) + has_e.astype(jnp.int32)
-    pl.semaphore_wait(barrier, near_r * near_c)
-
-    @pl.when(has_n)
-    def _():
-        each_tile(lambda k, t: row_copy(k, t, False).start())
-
-    @pl.when(has_s)
-    def _():
-        each_tile(lambda k, t: row_copy(k, t, True).start())
-
     def clear_rows(dest):
         for source, target, base in arrays:
             spot = pl.ds(base + dest, HALO)
@@ -132,7 +143,100 @@
         for q in range(3):
             vert[q, t, spot_g, :] = via[q, t, spot, :].astype(F32)
 
-    each_tile(lambda k, t: local_copy(k, t).wait())
+    loaded(0, 1, 2)
+
+    def from_east(v):
+        r = pltpu.roll(v, LANES - 1, 2)
+        return jnp.where(lane3 == LANES - 1, jnp.concatenate([r[1:], r[:1]], 0), r)
+
+    def from_west(v):
+        r = pltpu.roll(v, 1, 2)
+        return jnp.where(lane3 == 0, jnp.concatenate([r[-1:], r[:-1]], 0), r)
+
+    def at(first):
+        return pl.ds(first + GUARD, R)
+
+    strip_group = lane // 16
+
+    def heat_of(state, first, low, count):
+        heats = []
+        for p in range(4):
+            v = state[p, low : low + count, at(first), :]
+            follow = state[p, (low + count) % (tiles + 1), at(first), :][None]
+            r = pltpu.roll(jnp.concatenate([v, follow], 0), LANES - 1, 2)
+            de = v - jnp.where(lane3 == LANES - 1, r[1:], r[:-1])
+            ds = v - state[p, low : low + count, at(first + 1), :]
+            heats.append(cx[p, low : low + count, at(first), :] * (de * de)
+                         + cy[p, low : low + count, at(first), :] * (ds * ds))
+        return heats[0] + heats[3], heats[1] + heats[2]
+
+    def strip_of(planes):
+        full = jnp.zeros((8, LANES), F32)
+        for q in range(2):
+            for b in range(R // 8):
+                k = 2 * b + q
+                full = jnp.where(
+                    lane // 32 == k, pltpu.roll(planes[q][8 * b : 8 * b + 8], (8 + 32 * k) % LANES, 1), full)
+        return jnp.where(strip_group % 2 == 1, pltpu.roll(full[4:8], 16, 1), full[0:4])
+
+    def planes_of(strip):
+        full = jnp.concatenate([strip, pltpu.roll(strip, LANES - 16, 1)], 0)
+        return [
+            jnp.concatenate(
+                [pltpu.roll(full, (LANES - 8 - 32 * (2 * b + q)) % LANES, 1) for b in range(R // 8)], 0)
+            for q in range(2)
+        ]
+
+    half = tiles * R
+
+    def first_main(c):
+        first = pl.multiple_of(c * R, R)
+
+        @pl.when(is_elec)
+        def _():
+            heat = heat_of(x, first, 0, tiles)
+            for q in range(2):
+                send_main[c, q * half : (q + 1) * half, :] = heat[q].reshape(half, LANES)
+
+        @pl.when(jnp.logical_not(is_elec))
+        def _():
+            for q in range(2):
+                send_main[c, q * half : (q + 1) * half, :] = x[q, 0:tiles, at(first), :].reshape(half, LANES)
+
+    def first_strip(c):
+        first = pl.multiple_of(c * R, R)
+
+        @pl.when(is_elec)
+        def _():
+            heat = heat_of(x, first, tiles - 1, 2)
+            send_strip[c] = strip_of([jnp.where(lane == 120, pltpu.roll(h[0], LANES - 7, 1), h[1]) for h in heat])
+
+        @pl.when(jnp.logical_not(is_elec))
+        def _():
+            send_strip[c] = strip_of([x[q, tiles, at(first), :] for q in range(2)])
+
+    def main_copy(c):
+        return pltpu.make_async_remote_copy(
+            src_ref=send_main.at[c], dst_ref=recv_main.at[c],
+            send_sem=main_send_sem.at[0], recv_sem=main_recv_sem.at[c],
+            device_id={"field": 1 - field}, device_id_type=MESH,
+        )
+
+    strip_copy = pltpu.make_async_remote_copy(
+        src_ref=send_strip, dst_ref=recv_strip, send_sem=strip_sem.at[0], recv_sem=strip_sem.at[1],
+        device_id={"field": 1 - field}, device_id_type=MESH,
+    )
+
+    def loop(low, high, action):
+        def body(c, carry):
+            action(c)
+            return carry
+        lax.fori_loop(low, high, body, 0)
+
+    early = min(EARLY, chunks - 2)
+    loop(1, chunks - 1, first_main)
+
+    loaded(3, 4, 5)
 
     def prepare_tile(t, carry):
         def body(i, carry):
@@ -192,15 +296,28 @@
         def _():
             col_copy(side, dr).start()
 
+    near_r = 1 + has_n.astype(jnp.int32) + has_s.astype(jnp.int32)
+    near_c = 1 + has_w.astype(jnp.int32) + has_e.astype(jnp.int32)
+    pl.semaphore_wait(barrier, near_r * near_c)
     each_side(send_side, False)
 
+    @pl.when(has_n)
+    def _():
+        each_tile(lambda k, t: row_copy(k, t, False).start())
+
     @pl.when(has_s)
     def _():
-        each_tile(lambda k, t: row_copy(k, t, False).wait_recv())
+        each_tile(lambda k, t: row_copy(k, t, True).start())
+
+    loop(1, 1 + early, lambda c: main_copy(c).start())
+
+    @pl.when(has_s)
+    def _():
+        rows_done(row_recv_sem, False)
 
     @pl.when(has_n)
     def _():
-        each_tile(lambda k, t: row_copy(k, t, True).wait_recv())
+        rows_done(row_recv_sem, True)
 
     def prepare_edge(t, carry):
         prepare(0, HALO, t)
@@ -234,17 +351,6 @@
             ref[index] = jnp.where(lane < 64, e, w)
         return carry
     lax.fori_loop(0, chunks, unpack, 0)
-
-    def from_east(v):
-        r = pltpu.roll(v, LANES - 1, 2)
-        return jnp.where(lane3 == LANES - 1, jnp.concatenate([r[1:], r[:1]], 0), r)
-
-    def from_west(v):
-        r = pltpu.roll(v, 1, 2)
-        return jnp.where(lane3 == 0, jnp.concatenate([r[-1:], r[:-1]], 0), r)
-
-    def at(first):
-        return pl.ds(first + GUARD, R)
 
     def half_east():
         tile = lax.broadcasted_iota(jnp.int32, (tiles + 1, 1, LANES), 0)
@@ -299,57 +405,45 @@
                     total = total + src[p, :, at(first), :]
             new[p, :, at(first), :] = total * rw[p, :, at(first), :]
 
-    strip_group = lane // 16
-
-    def write_map(step, c, planes):
-        strip = jnp.zeros((STRIP, LANES), F32)
-        for q in range(2):
-            send_map[step, c, pl.ds(q * tiles * R, tiles * R), :] = planes[q][:tiles].reshape(tiles * R, LANES)
-            for b in range(R // 8):
-                k = 2 * b + q
-                strip = jnp.where(
-                    strip_group == k, pltpu.roll(planes[q][tiles, 8 * b : 8 * b + 8], 8 + 16 * k, 1), strip)
-        send_map[step, c, pl.ds(2 * tiles * R, STRIP), :] = strip
-
-    def read_map(step, c):
-        strip = recv_map[step, c, pl.ds(2 * tiles * R, STRIP), :]
-        planes = []
-        for q in range(2):
-            main = recv_map[step, c, pl.ds(q * tiles * R, tiles * R), :].reshape(tiles, R, LANES)
-            parts = [pltpu.roll(strip, LANES - (8 + 16 * (2 * b + q)), 1) for b in range(R // 8)]
-            planes.append(jnp.concatenate([main, jnp.concatenate(parts, 0)[None]], 0))
-        return planes
-
-    def map_copy(step, c):
+    def send_chunk(c, state):
+        first = pl.multiple_of(c * R, R)
+
+        def write(planes):
+            for q in range(2):
+                send_map[c, q * half : (q + 1) * half, :] = planes[q][:tiles].reshape(half, LANES)
+            send_map[c, 2 * half : 2 * half + STRIP, :] = strip_of([planes[q][tiles] for q in range(2)])
+
+        @pl.when(is_elec)
+        def _():
+            write(heat_of(state, first, 0, tiles + 1))
+
+        @pl.when(jnp.logical_not(is_elec))
+        def _():
+            write((state[0, :, at(first), :], state[1, :, at(first), :]))
+
+        map_copy(c).start()
+
+    def map_copy(c):
         return pltpu.make_async_remote_copy(
-            src_ref=send_map.at[step, c], dst_ref=recv_map.at[step, c],
-            send_sem=map_send_sem.at[step, c], recv_sem=map_recv_sem.at[step, c],
+            src_ref=send_map.at[c], dst_ref=recv_map.at[c],
+            send_sem=map_send_sem.at[c], recv_sem=map_recv_sem.at[c],
             device_id={"field": 1 - field}, device_id_type=MESH,
         )
 
-    def send_chunk(step, c, state):
-        first = pl.multiple_of(c * R, R)
-
-        @pl.when(is_elec)
-        def _():
-            heats = []
-            for p in range(4):
-                v = state[p, :, at(first), :]
-                de = v - from_east(v)
-                ds = v - state[p, :, at(first + 1), :]
-                heats.append(cx[p, :, at(first), :] * (de * de) + cy[p, :, at(first), :] * (ds * ds))
-            write_map(step, c, (heats[0] + heats[3], heats[1] + heats[2]))
-
-        @pl.when(jnp.logical_not(is_elec))
-        def _():
-            write_map(step, c, (state[0, :, at(first), :], state[1, :, at(first), :]))
-
-        map_copy(step, c).start()
-
-    def first_maps(c, carry):
-        send_chunk(0, c, x)
-        return carry
-    lax.fori_loop(0, chunks, first_maps, 0)
+    def read_map(step, c):
+        source = recv_map if step else recv_main
+        strip = recv_map[c, 2 * half : 2 * half + STRIP, :] if step else recv_strip[c]
+        return [
+            jnp.concatenate([source[c, q * half : (q + 1) * half, :].reshape(tiles, R, LANES), edge[None]], 0)
+            for q, edge in enumerate(planes_of(strip))
+        ]
+
+    first_main(0)
+    loop(0, chunks, first_strip)
+    main_copy(0).start()
+    strip_copy.start()
+    first_main(chunks - 1)
+    loop(1 + early, chunks, lambda c: main_copy(c).start())
 
     @pl.when(jnp.logical_not(is_elec))
     def _():
@@ -365,7 +459,7 @@
 
     def advance(step, c, buffers):
         first = pl.multiple_of(c * R, R)
-        map_copy(step, c).wait_recv()
+        (map_copy if step else main_copy)(c).wait_recv()
 
         @pl.when(is_elec)
         def _():
@@ -384,11 +478,17 @@
         @pl.when(jnp.logical_not(is_elec))
         def _():
             joule = read_map(step, c)
+            if step == 0:
+                tile = lax.broadcasted_iota(jnp.int32, (tiles + 1, 1, LANES), 0)
+                last = (tile == tiles - 1) & (lane3 == LANES - 1)
+                joule = [jnp.where(last, pltpu.roll(j[tiles:], 7, 2), j) for j in joule]
             src[0, :, at(first), :] = joule[0]
             src[1, :, at(first), :] = joule[1] + load[:, at(first), :]
             for s in range(SWEEPS):
                 sweep(buffers[s], buffers[s + 1], first - 1 - s, False)
 
+    strip_copy.wait_recv()
+
     def step_one(c, carry):
         @pl.when(c < chunks)
         def _():
@@ -396,7 +496,7 @@
 
         @pl.when(c > 0)
         def _():
-            send_chunk(1, c - 1, z)
+            send_chunk(c - 1, z)
         return carry
     lax.fori_loop(0, chunks + 1, step_one, 0)
 
@@ -404,7 +504,7 @@
         return pltpu.make_async_copy(
             x.at[:, t, pl.ds(pl.multiple_of(c * R + GUARD + HALO, 8), R), :],
             out.at[0, :, pl.ds(pl.multiple_of(c * R, R), R), lanes_of(t)],
-            out_sem.at[c, t],
+            out_sem.at[0],
         )
 
     def step_two(c, carry):
@@ -417,24 +517,18 @@
         return carry
     lax.fori_loop(0, chunks, step_two, 0)
 
-    def finish(c, carry):
-        for step in range(STEPS):
-            map_copy(step, c).wait_send()
-
-        @pl.when(c > 0)
-        def _():
-            for t in range(tiles):
-                out_copy(c - 1, t).wait()
-        return carry
-    lax.fori_loop(0, chunks, finish, 0)
+    wait_for(out, out_sem.at[0])
+    wait_for(send_main, main_send_sem.at[0])
+    strip_copy.wait_send()
+    loop(0, chunks, lambda c: map_copy(c).wait_send())
 
     @pl.when(has_n)
     def _():
-        each_tile(lambda k, t: row_copy(k, t, False).wait_send())
+        rows_done(row_send_sem, False)
 
     @pl.when(has_s)
     def _():
-        each_tile(lambda k, t: row_copy(k, t, True).wait_send())
+        rows_done(row_send_sem, True)
 
     def sent_side(side, dr, there):
         @pl.when(there)
@@ -451,7 +545,6 @@
     chunks = wide // R
     tall = wide + 2 * GUARD
     field = pltpu.VMEM((4, tiles + 1, tall, LANES), F32)
-    message = 2 * tiles * R + STRIP
     dma = pltpu.SemaphoreType.DMA
     hbm = pl.BlockSpec(memory_space=pl.ANY)
     return pl.pallas_call(
@@ -468,12 +561,13 @@
             pltpu.VMEM((tiles, wide, LANES), F32),
             pltpu.VMEM((tiles, wide, LANES), jnp.int32),
             pltpu.VMEM((3, tiles, wide, LANES), jnp.int32),
-            pltpu.VMEM((STEPS, chunks, message, LANES), F32),
-            pltpu.VMEM((STEPS, chunks, message, LANES), F32),
+            *[pltpu.VMEM((chunks, 2 * tiles * R, LANES), F32)] * 2,
+            *[pltpu.VMEM((chunks, STRIP, LANES), F32)] * 2,
+            *[pltpu.VMEM((chunks, 2 * tiles * R + STRIP, LANES), F32)] * 2,
             pltpu.VMEM((2, rows, LANES), F32),
             pltpu.VMEM((2, wide, LANES), F32),
-            dma((6, tiles)), dma((2, 6, tiles)), dma((2, 6, tiles)), dma((2, 3)), dma((2, 3)),
-            dma((STEPS, chunks)), dma((STEPS, chunks)), dma((chunks, tiles)),
+            dma((6,)), dma((2, 6)), dma((2, 6)), dma((2, 3)), dma((2, 3)),
+            dma((1,)), dma((chunks,)), dma((2,)), dma((chunks,)), dma((chunks,)), dma((1,)),
         ],
         compiler_params=pltpu.CompilerParams(
             collective_id=0, has_side_effects=True, vmem_limit_bytes=60 * 1024 * 1024

time: 77.3 us -> 71.3 us (0.922)
  the two profiles are of different devices: /device:TPU:25 before, /device:TPU:7 now
where the time goes in v2:
time: 71.3 us; the launch traced here: 71.1 us
  Pallas kernels  68 us (95%)
  local copies, waits for them, and re-layouts  3.08 us (4%)
    pallas_call x1, Pallas kernels, shards(): pl.pallas_call(functools.partial(kernel, grid_rows, grid_cols), name='cou...  68 us
    unnamed x1, local copies, waits for them, and re-layouts  3.08 us

profile of v2, /device:TPU:7, one launch (start us, length us, event | category | flops | bytes accessed | tf_op | source)
XLA Modules:
  0.0 71.1 jit_solution(4393269605294343471)
XLA Ops:
  0.0 68.0 %coupled_sweeps.1 = f32[1,4,256,512]{3,2,1,0:T(8,128)} custom-call(f32[1,4,256,512]{3,2,1,0:T(8,128)} %state_in.1, f32[1,4,256,512]{3,2,1,0:T(8,128)} %cx_in.1, f32[1,4,256,512]{3,2,1,0:T(8,128)} %cy_in.1, f32[1,256,512]{2,1,0:T(8,128)} %act_in.1, s32[1,256,512]{2,1,0:T(8,128)} %class_in.1, f32[1,8]{1,0:T(1,128)} %table.1, s32[1,3,256,512]{3,2,1,0:T(8,128)} %via_in.1), custom_call_target="tpu_custom_call" | custom-call | tf_op jit(solution)/shard_map/coupled_sweeps/pallas_call | solution.py:550
  68.0 3.1 %copy.9 = f32[1,4,256,512]{3,2,1,0:T(8,128)} copy(f32[1,4,256,512]{3,2,1,0:T(8,128)} %coupled_sweeps.1) | data formatting | bytes 4194304

commit v3 on v2

--- a/solution.py
+++ b/solution.py
@@ -1,4 +1,5 @@
 import functools
+import math
 
 import jax
 import jax.numpy as jnp
@@ -19,6 +20,8 @@
 R = 16
 STRIP = 4
 EARLY = 6
+FIRST = 4
+GROUP = 6
 PACKED = 16
 
 
@@ -153,21 +156,21 @@
         r = pltpu.roll(v, 1, 2)
         return jnp.where(lane3 == 0, jnp.concatenate([r[-1:], r[:-1]], 0), r)
 
-    def at(first):
-        return pl.ds(first + GUARD, R)
+    def at(first, count=R):
+        return pl.ds(first + GUARD, count)
 
     strip_group = lane // 16
 
-    def heat_of(state, first, low, count):
+    def heat_of(state, first, low, count, n=R):
         heats = []
         for p in range(4):
-            v = state[p, low : low + count, at(first), :]
-            follow = state[p, (low + count) % (tiles + 1), at(first), :][None]
+            v = state[p, low : low + count, at(first, n), :]
+            follow = state[p, (low + count) % (tiles + 1), at(first, n), :][None]
             r = pltpu.roll(jnp.concatenate([v, follow], 0), LANES - 1, 2)
             de = v - jnp.where(lane3 == LANES - 1, r[1:], r[:-1])
-            ds = v - state[p, low : low + count, at(first + 1), :]
-            heats.append(cx[p, low : low + count, at(first), :] * (de * de)
-                         + cy[p, low : low + count, at(first), :] * (ds * ds))
+            ds = v - state[p, low : low + count, at(first + 1, n), :]
+            heats.append(cx[p, low : low + count, at(first, n), :] * (de * de)
+                         + cy[p, low : low + count, at(first, n), :] * (ds * ds))
         return heats[0] + heats[3], heats[1] + heats[2]
 
     def strip_of(planes):
@@ -203,17 +206,26 @@
             for q in range(2):
                 send_main[c, q * half : (q + 1) * half, :] = x[q, 0:tiles, at(first), :].reshape(half, LANES)
 
-    def first_strip(c):
-        first = pl.multiple_of(c * R, R)
+    def first_strips():
+        group = min(GROUP, chunks)
+        starts = [min(c, chunks - group) for c in range(0, chunks, group)]
+
+        def make(planes_at):
+            for start in starts:
+                planes = planes_at(start * R, group * R)
+                for c in range(group):
+                    send_strip[start + c] = strip_of([plane[c * R : (c + 1) * R] for plane in planes])
 
         @pl.when(is_elec)
         def _():
-            heat = heat_of(x, first, tiles - 1, 2)
-            send_strip[c] = strip_of([jnp.where(lane == 120, pltpu.roll(h[0], LANES - 7, 1), h[1]) for h in heat])
+            def edges(first, n):
+                heat = heat_of(x, first, tiles - 1, 2, n)
+                return [jnp.where(lane == 120, pltpu.roll(h[0], LANES - 7, 1), h[1]) for h in heat]
+            make(edges)
 
         @pl.when(jnp.logical_not(is_elec))
         def _():
-            send_strip[c] = strip_of([x[q, tiles, at(first), :] for q in range(2)])
+            make(lambda first, n: [x[q, tiles, at(first, n), :] for q in range(2)])
 
     def main_copy(c):
         return pltpu.make_async_remote_copy(
@@ -234,7 +246,8 @@
         lax.fori_loop(low, high, body, 0)
 
     early = min(EARLY, chunks - 2)
-    loop(1, chunks - 1, first_main)
+    ready = min(FIRST, early)
+    loop(1, 1 + ready, first_main)
 
     loaded(3, 4, 5)
 
@@ -258,21 +271,23 @@
 
     group = lane // 8
 
+    deep = math.gcd(rows, 64)
+
     def pack(i, carry):
-        first = pl.multiple_of(i * 32, 32)
-        spot = pl.ds(first + GUARD + HALO, 32)
-        west = jnp.zeros((32, LANES), F32)
-        east = jnp.zeros((32, LANES), F32)
+        first = pl.multiple_of(i * deep, deep)
+        spot = pl.ds(first + GUARD + HALO, deep)
+        west = jnp.zeros((deep, LANES), F32)
+        east = jnp.zeros((deep, LANES), F32)
         for q in range(PACKED):
             ref, index = plane_at(q, 0, spot)
             west = jnp.where(group == q, pltpu.roll(ref[index], 8 * q, 1) if q else ref[index], west)
             ref, index = plane_at(q, tiles - 1, spot)
             shift = (8 * q + 8) % LANES
             east = jnp.where(group == q, pltpu.roll(ref[index], shift, 1) if shift else ref[index], east)
-        pack_send[0, pl.ds(first, 32), :] = west
-        pack_send[1, pl.ds(first, 32), :] = east
+        pack_send[0, pl.ds(first, deep), :] = west
+        pack_send[1, pl.ds(first, deep), :] = east
         return carry
-    lax.fori_loop(0, rows // 32, pack, 0)
+    lax.fori_loop(0, rows // deep, pack, 0)
 
     def col_copy(side, dr):
         first, dest, count = ((0, rows + HALO, HALO), (0, HALO, rows), (rows - HALO, 0, HALO))[dr + 1]
@@ -300,6 +315,7 @@
     near_c = 1 + has_w.astype(jnp.int32) + has_e.astype(jnp.int32)
     pl.semaphore_wait(barrier, near_r * near_c)
     each_side(send_side, False)
+    loop(1, 1 + ready, lambda c: main_copy(c).start())
 
     @pl.when(has_n)
     def _():
@@ -309,7 +325,8 @@
     def _():
         each_tile(lambda k, t: row_copy(k, t, True).start())
 
-    loop(1, 1 + early, lambda c: main_copy(c).start())
+    loop(1 + ready, chunks - 1, first_main)
+    loop(1 + ready, 1 + early, lambda c: main_copy(c).start())
 
     @pl.when(has_s)
     def _():
@@ -338,19 +355,19 @@
 
     each_side(recv_side, True)
 
-    def unpack(c, carry):
-        first = pl.multiple_of(c * R, R)
-        spot = pl.ds(first + GUARD, R)
-        east = pack_recv[0, pl.ds(first, R), :]
-        west = pack_recv[1, pl.ds(first, R), :]
+    def unpack(first, n):
+        spot = pl.ds(first + GUARD, n)
+        east = pack_recv[0, pl.ds(first, n), :]
+        west = pack_recv[1, pl.ds(first, n), :]
         for q in range(PACKED):
             e = pltpu.roll(east, LANES - 8 * q, 1) if q else east
             shift = (120 - 8 * q) % LANES
             w = pltpu.roll(west, shift, 1) if shift else west
             ref, index = plane_at(q, tiles, spot)
             ref[index] = jnp.where(lane < 64, e, w)
-        return carry
-    lax.fori_loop(0, chunks, unpack, 0)
+
+    loop(0, rows // deep, lambda i: unpack(pl.multiple_of(i * deep, deep), deep))
+    unpack(rows, 2 * HALO)
 
     def half_east():
         tile = lax.broadcasted_iota(jnp.int32, (tiles + 1, 1, LANES), 0)
@@ -439,7 +456,7 @@
         ]
 
     first_main(0)
-    loop(0, chunks, first_strip)
+    first_strips()
     main_copy(0).start()
     strip_copy.start()
     first_main(chunks - 1)

time: 71.3 us -> 66.7 us (0.935)
  the two profiles are of different devices: /device:TPU:7 before, /device:TPU:25 now
where the time goes in v3:
time: 66.7 us; the launch traced here: 65.6 us
  Pallas kernels  62.6 us (94%)
  local copies, waits for them, and re-layouts  3.08 us (5%)
    pallas_call x1, Pallas kernels, shards(): pl.pallas_call(functools.partial(kernel, grid_rows, grid_cols), name='cou...  62.6 us
    unnamed x1, local copies, waits for them, and re-layouts  3.08 us

profile of v3, /device:TPU:25, one launch (start us, length us, event | category | flops | bytes accessed | tf_op | source)
XLA Modules:
  0.0 65.6 jit_solution(5581029893336538283)
XLA Ops:
  0.0 62.6 %coupled_sweeps.1 = f32[1,4,256,512]{3,2,1,0:T(8,128)} custom-call(f32[1,4,256,512]{3,2,1,0:T(8,128)} %state_in.1, f32[1,4,256,512]{3,2,1,0:T(8,128)} %cx_in.1, f32[1,4,256,512]{3,2,1,0:T(8,128)} %cy_in.1, f32[1,256,512]{2,1,0:T(8,128)} %act_in.1, s32[1,256,512]{2,1,0:T(8,128)} %class_in.1, f32[1,8]{1,0:T(1,128)} %table.1, s32[1,3,256,512]{3,2,1,0:T(8,128)} %via_in.1), custom_call_target="tpu_custom_call" | custom-call | tf_op jit(solution)/shard_map/coupled_sweeps/pallas_call | solution.py:567
  62.6 3.1 %copy.9 = f32[1,4,256,512]{3,2,1,0:T(8,128)} copy(f32[1,4,256,512]{3,2,1,0:T(8,128)} %coupled_sweeps.1) | data formatting | bytes 4194304
